TPU v7x, 256 devices: a whole 4x4x8 slice. The times are simulated.
256 devices in a mesh: row: 32 (over z_lo, x, core), col: 8 (over z_hi, y).
Axes of the slice: x: 4, y: 4, z: 8 (z_hi: 2, z_lo: 4; z = z_hi * 4 + z_lo), core: 2. Of those that a mesh axis runs over, the one named last changes fastest.
Arguments:
- right_sides: float32 [16384, 1024], P('row', 'col'), may hold values from -6 to 6
- pencil_s: float32 [16384, 512], P('row'), as said below
- pencil_t: float32 [16384, 512], P('row'), as said below
- value_alpha: float32 [4096], replicated, may hold values from -3 to -0.5
- value_beta: float32 [4096], replicated, may hold values from 0.5 to 1
- selected: int32 [1024], P('col'), may hold values from 0 to 4095
- block_slot: int32 [64], replicated, may hold values from 0 to 63, as said below
- right_basis: float32 [65536, 2, 256], P('row', None, 'col'), may hold values from -0.25 to 0.25
- vectors: float32 [65536, 1024], P('row', 'col'), may hold values from -6 to 6
Outputs:
- updated_sides: float32 [16384, 1024], P('row', 'col')
- updated_vectors: float32 [65536, 1024], P('row', 'col')
Inputs may be any that keep to these rules, and one draw needn't show every extreme that they name: A permutation: logical block b of 256 rows is stored at slot block_slot[b]. `pencil_s`: in the window, entries left of the diagonal are 0 and diagonal entries lie in [1, 2]. `pencil_t`: in the window, entries left of the diagonal are 0 and diagonal entries lie in [1, 2].
All inputs are finite; a program needn't handle non-finite values.
Results may differ from a plain program's by a relative error of at most 0.0003.
Values sent between devices are 32-bit elements; how exact they have to be, the bound alone decides.
A program may use at most 64 MiB of HBM per device.

v0:
```python
import jax
import jax.numpy as jnp
from jax import lax
from jax.sharding import PartitionSpec as P

BLK = 256
LEAD_DEV = 512


exact_mode = lax.Precision.HIGHEST
sub_rows = 32


def from_root(block, axis, source):
    block = jnp.where(lax.axis_index(axis) == source, block, jnp.zeros_like(block))
    return lax.psum(block, axis)


def table_lookup(selected, table):
    positions = lax.broadcasted_iota(jnp.int32, (table.shape[0], selected.shape[0]), 0)
    return jnp.sum(jnp.where(positions == selected[None, :], table[:, None], 0.0), axis=0)


def shifted_apply(s_cols, t_cols, solved, shift_alpha, shift_beta):
    first_term = jnp.dot(
        s_cols,
        solved * shift_beta[None, :],
        precision=exact_mode,
        preferred_element_type=jnp.float32,
    )
    second_term = jnp.dot(
        t_cols,
        solved * shift_alpha[None, :],
        precision=exact_mode,
        preferred_element_type=jnp.float32,
    )
    return first_term - second_term


def solve_block(s_diag, t_diag, right, shift_alpha, shift_beta):
    size_rows = s_diag.shape[0]
    upper_mask = lax.broadcasted_iota(jnp.int32, s_diag.shape, 0) <= lax.broadcasted_iota(
        jnp.int32, s_diag.shape, 1
    )
    s_upper = jnp.where(upper_mask, s_diag, 0.0)
    t_upper = jnp.where(upper_mask, t_diag, 0.0)
    turn_count = size_rows // sub_rows

    def one_turn(step, carry):
        remaining, solved_all = carry
        first_row = (turn_count - 1 - step) * sub_rows
        s_small = lax.dynamic_slice(s_upper, (first_row, first_row), (sub_rows, sub_rows))
        t_small = lax.dynamic_slice(t_upper, (first_row, first_row), (sub_rows, sub_rows))
        combined = (
            shift_beta[None, None, :] * s_small[:, :, None]
            - shift_alpha[None, None, :] * t_small[:, :, None]
        )
        pending = lax.dynamic_slice_in_dim(remaining, first_row, sub_rows, 0)
        entries = [None] * sub_rows
        for column in reversed(range(sub_rows)):
            entry_value = pending[column] / combined[column, column]
            entries[column] = entry_value
            pending = pending - combined[:, column, :] * entry_value[None, :]
        solved_small = jnp.stack(entries)
        s_cols = lax.dynamic_slice_in_dim(s_upper, first_row, sub_rows, 1)
        t_cols = lax.dynamic_slice_in_dim(t_upper, first_row, sub_rows, 1)
        remaining = remaining - shifted_apply(s_cols, t_cols, solved_small, shift_alpha, shift_beta)
        solved_all = lax.dynamic_update_slice_in_dim(solved_all, solved_small, first_row, 0)
        return (remaining, solved_all)

    _, solved_all = lax.fori_loop(0, turn_count, one_turn, (right, jnp.zeros_like(right)))
    return solved_all


def block_term(basis_cols, solved):
    matched_rows = lax.all_to_all(solved, "col", split_axis=0, concat_axis=1, tiled=True)
    partial_value = jnp.dot(
        basis_cols, matched_rows, precision=exact_mode, preferred_element_type=jnp.float32
    )
    return lax.psum_scatter(partial_value, "col", scatter_dimension=1, tiled=True)


def on_device(
    right_sides,
    pencil_s,
    pencil_t,
    value_alpha,
    value_beta,
    selected,
    block_slot,
    right_basis,
    vectors,
):
    shift_alpha = table_lookup(selected, value_alpha)
    shift_beta = table_lookup(selected, value_beta)
    slot_count = LEAD_DEV // BLK
    local_eigs = right_sides.shape[1]
    block_count = block_slot.shape[0]
    slot_upper = block_slot[block_count - 2]
    slot_lower = block_slot[block_count - 1]
    s_view = pencil_s.reshape(slot_count, BLK, 2 * BLK)
    t_view = pencil_t.reshape(slot_count, BLK, 2 * BLK)
    side_view = right_sides.reshape(slot_count, BLK, local_eigs)

    def pick_slot(view, slot_index):
        return lax.dynamic_index_in_dim(view, slot_index % slot_count, 0, keepdims=False)

    s_lower = pick_slot(s_view, slot_lower)
    t_lower = pick_slot(t_view, slot_lower)
    lower_local = solve_block(
        s_lower[:, BLK:],
        t_lower[:, BLK:],
        pick_slot(side_view, slot_lower),
        shift_alpha,
        shift_beta,
    )
    solved_lower = from_root(lower_local, "row", slot_lower // slot_count)
    s_upper = pick_slot(s_view, slot_upper)
    t_upper = pick_slot(t_view, slot_upper)
    right_upper = pick_slot(side_view, slot_upper) - shifted_apply(
        s_upper[:, BLK:], t_upper[:, BLK:], solved_lower, shift_alpha, shift_beta
    )
    upper_local = solve_block(
        s_upper[:, :BLK], t_upper[:, :BLK], right_upper, shift_alpha, shift_beta
    )
    solved_upper = from_root(upper_local, "row", slot_upper // slot_count)
    window_x = jnp.concatenate([solved_upper, solved_lower], 0)
    updated = right_sides - shifted_apply(pencil_s, pencil_t, window_x, shift_alpha, shift_beta)
    global_slot = lax.axis_index("row") * slot_count + lax.broadcasted_iota(
        jnp.int32, (slot_count,), 0
    )
    updated_view = updated.reshape(slot_count, BLK, local_eigs)
    updated_view = jnp.where(
        (global_slot == slot_upper)[:, None, None], solved_upper[None], updated_view
    )
    updated_view = jnp.where(
        (global_slot == slot_lower)[:, None, None], solved_lower[None], updated_view
    )
    updated_sides = updated_view.reshape(LEAD_DEV, local_eigs)
    updated_vectors = (
        vectors
        + block_term(right_basis[:, 0, :], solved_upper)
        + block_term(right_basis[:, 1, :], solved_lower)
    )
    return (updated_sides, updated_vectors)


def solution(mesh):
    return jax.shard_map(
        on_device,
        mesh=mesh,
        in_specs=(
            P("row", "col"),
            P("row", None),
            P("row", None),
            P(),
            P(),
            P("col"),
            P(),
            P("row", None, "col"),
            P("row", "col"),
        ),
        out_specs=(P("row", "col"), P("row", "col")),
        check_vma=False,
    )
```

profile of v0, /device:TPU:1, one launch (start us, length us, event | category | flops | bytes accessed | tf_op | source)
XLA Modules:
  0.0 968.4 jit_solution(17689833058718998711)
XLA Ops:
  7.2 1.4 fusion.231
  13.2 1.7 constant_dynamic-slice_fusion.2
  15.9 2.2 select_reduce_fusion
  18.1 18.8 %while.30 = (s32[]{:T(128)}, f32[256,128]{1,0:T(8,128)S(1)}, f32[256,128]{1,0:T(8,128)S(1)}, f32[256,256]{0,1:T(8,128)S(1)}, f32[128]{0:T(128)S(1)}, /*index=5*/...) while((s32[]{:T(128)}, f32[256,128]{1,0:T(8,128)S(1)}, ...), condition=%wide.region_3.4_spmd, body=%wide.region_2.3_spmd.sunk | while | flops 25882888 | bytes 2812127 | solution.py:71
  36.9 0.7 broadcast_select_fusion.1
  38.7 258.4 %all-reduce.3.cloned.1.call-done = f32[256,128]{1,0:T(8,128)} async-done(((f32[256,128]{1,0:T(8,128)}), f32[256,128]{1,0:T(8,128)}) %all-reduce.3.cloned.1.call-update) | async-done | bytes 131088 | tf_op jit(solution)/shard_map/psum | solution.py:16
  297.0 1.5 fusion.210
  298.5 1.5 fusion.208
  300.1 18.8 %while.31 = (s32[]{:T(128)}, f32[256,128]{1,0:T(8,128)S(1)}, f32[256,128]{1,0:T(8,128)S(1)}, f32[256,256]{0,1:T(8,128)S(1)}, f32[128]{0:T(128)S(1)}, /*index=5*/...) while((s32[]{:T(128)}, f32[256,128]{1,0:T(8,128)S(1)}, ...), condition=%wide.region_6.7_spmd, body=%wide.region_5.6_spmd.sunk | while | flops 25882888 | bytes 2812127 | solution.py:71
  318.8 7.3 all-to-all-start.1
  326.2 0.7 broadcast_select_fusion
  327.0 8.5 all-to-all-done.1
  335.5 9.0 convolution_bitcast_fusion
  344.6 243.6 %all-reduce.5.cloned.1.call-done = f32[256,128]{1,0:T(8,128)} async-done(((f32[256,128]{1,0:T(8,128)}), f32[256,128]{1,0:T(8,128)}) %all-reduce.5.cloned.1.call-update) | async-done | bytes 131088 | tf_op jit(solution)/shard_map/psum | solution.py:16
  588.2 16.7 %all_to_all.38 = f32[8,32,128]{2,1,0:T(8,128)S(1)} all-to-all(f32[8,32,128]{2,1,0:T(8,128)} %bitcast.1125), channel_id=1, replica_groups=mesh['row'=32,'col'=8] {'col'}, dimensions={0} | all-to-all | bytes 262144 | tf_op jit(solution)/shard_map/all_to_all | solution.py:76
  604.9 9.0 convolution_bitcast_fusion.1
  613.9 0.8 copy.51
  614.8 0.5 copy-done.3
  615.6 1.3 fusion.229
  617.0 1.7 copy.47
  618.7 1.1 broadcast_in_dim.304
  619.8 0.7 copy.63
  620.5 0.7 copy.50
  621.3 1.0 broadcast_in_dim.309
  622.4 0.9 constant_dynamic-update-slice_fusion.2
  623.3 1.2 fusion.217
  624.6 2.2 fusion.207
  626.8 0.8 copy.55
  627.6 149.2 %reduce-scatter.5.cloned.1.call-done = f32[2048,128]{0,1:T(8,128)} async-done(((f32[2048,1024]{0,1:T(8,128)}), f32[2048,128]{0,1:T(8,128)}) %reduce-scatter.5.cloned.1.call-update) | async-done | bytes 1048592 | tf_op jit(solution)/shard_map/reduce_scatter | solution.py:80
  776.8 182.1 %reduce-scatter.3.cloned.1.call-done = f32[2048,128]{0,1:T(8,128)} async-done(((f32[2048,1024]{0,1:T(8,128)}), f32[2048,128]{0,1:T(8,128)}) %reduce-scatter.3.cloned.1.call-update) | async-done | bytes 1048592 | tf_op jit(solution)/shard_map/reduce_scatter | solution.py:80
  958.9 1.7 add_add_fusion
  960.6 1.3 copy.56
  (1165 shorter events, 31.3 us)
Async XLA Ops:
  7.2 289.9 %all-reduce.3.cloned.1.call-start = ((), (), s32[]{:S(2)}) async-start(), calls=%async_computation.4 | async-start | bytes 262144 | tf_op jit(solution)/shard_map/psum | solution.py:16
  14.9 1.0 copy-start.4
  14.9 1.0 copy-start.7
  14.9 1.0 copy-start.8
  14.9 1.0 copy-start.9
  300.0 35.5 %copy-start.6 = (f32[2048,2,32]{0,2,1:T(8,128)S(1)}, f32[2048,2,32]{0,2,1:T(8,128)}, u32[]{:S(2)}) copy-start(f32[2048,2,32]{0,2,1:T(8,128)} %param.20) | copy-start | bytes 1572868
  318.8 16.7 %all-to-all-start.1 = ((f32[8,32,128]{2,1,0:T(8,128)}), f32[8,32,128]{2,1,0:T(8,128)S(1)}, u32[]{:S(2)}, u32[]{:S(2)}) async-start(f32[8,32,128]{2,1,0:T(8,128)} %bitcast.204), calls=%async_computation.2 | async-start | bytes 262144 | tf_op jit(solution)/shard_map/all_to_all | solution.py:76
  326.2 262.0 %all-reduce.5.cloned.1.call-start = ((), (), s32[]{:S(2)}) async-start(), calls=%async_computation.5 | async-start | bytes 262144 | tf_op jit(solution)/shard_map/psum | solution.py:16
  326.9 449.9 %reduce-scatter.5.cloned.1.call-start = ((), (), s32[]{:S(2)}) async-start(), calls=%async_computation.7 | async-start | bytes 9437184 | tf_op jit(solution)/shard_map/reduce_scatter | solution.py:80
  344.6 614.3 %reduce-scatter.3.cloned.1.call-start = ((), (), s32[]{:S(2)}) async-start(), calls=%async_computation.6 | async-start | bytes 9437184 | tf_op jit(solution)/shard_map/reduce_scatter | solution.py:80
  613.9 1.3 copy-start.3
  613.9 6.6 copy-start.2
  615.2 8.1 copy-start
  618.7 5.8 copy-start.1
  621.3 3.3 copy-start.5
Sparse Core Ops, SparseCore 0:
  37.7 259.2 all-reduce.2
  330.2 257.9 all-reduce.4
  592.4 184.3 reduce-scatter.4
  780.8 177.9 reduce-scatter.2
where the time goes:
time: 970 us; the launch traced here: 968 us
  waiting for transfers between devices  842 us (87%)
  matrix products  37.3 us (4%)
  between operations  19.3 us (2%)
  local copies, waits for them, and re-layouts  18.7 us (2%)
  other arithmetic  18.7 us (2%)
  blocking collectives  16.7 us (2%)
    psum x2, waiting for transfers between devices, from_root(): return lax.psum(block, axis)  502 us
    reduce_scatter x2, waiting for transfers between devices, block_term(): lax.psum_scatter(partial_value, 'col', scatter_dimension=1, tiled=True)  331 us
  transfers between devices with their start and end apart: 5, of which 5 were waited for; matrix products, arithmetic and copies ran while one was open for 3% of the time, Pallas kernels for 0%

commit v1 on v0

v1 whole, which is shorter than its diff:
```python
import functools

import jax
import jax.numpy as jnp
from jax import lax
from jax.experimental import pallas as pl
from jax.experimental.pallas import tpu as pltpu
from jax.sharding import PartitionSpec as P

MESH = pl.DeviceIdType.MESH
BLK = 256
SUB = 32
PANELS = BLK // SUB
NCH = 8
CH = 64 // NCH
ORD = 2048
F32 = jnp.float32
BF = jnp.bfloat16
FIRST_Z = 3


def split(v):
    hi = v.astype(BF)
    return hi, (v - hi.astype(F32)).astype(BF)


def dot(a, b):
    return jnp.dot(a, b, preferred_element_type=F32)


def dot3(a, b):
    ah, al = split(a)
    bh, bl = split(b)
    return dot(ah, bh) + (dot(ah, bl) + dot(al, bh))


def kernel(
    slot_ref, alpha_ref, beta_ref, sel_ref, side_hbm, s_hbm, t_hbm, zt,
    out_side, out_vec,
    side_ref, s_ref, t_ref, zbuf, sd, td, lmat, rbuf, cand, st1, st2, xw, xpad, coef, shifts,
    zr, zs, s1r, s1s, s2r, s2s, s3r, s3s, lsem,
):
    row = lax.axis_index("row")
    col = lax.axis_index("col")
    zlo = row // 8
    pi = row % 8
    zh = col // 4
    y = col % 4
    yp, ym, y2 = (y + 1) % 4, (y + 3) % 4, (y + 2) % 4
    oh = 1 - zh

    loads = []
    for n, (src, dst) in enumerate(((s_hbm, s_ref), (t_hbm, t_ref), (side_hbm, side_ref), (zt, zbuf.at[col]))):
        loads.append(pltpu.make_async_copy(src, dst, lsem.at[n]))
        loads[-1].start()

    bar = pltpu.get_barrier_semaphore()
    peers = [(row, zh * 4 + yp), (row, zh * 4 + ym), (row, oh * 4 + y)]
    peers += [(zlo * 8 + (pi + d) % 8, col) for d in range(1, 8)]
    peers += [(((zlo + d) % 4) * 8 + pi, col) for d in range(1, 4)]
    for d in peers:
        pl.semaphore_signal(bar, inc=1, device_id=d, device_id_type=MESH)
    pl.semaphore_wait(bar, len(peers))

    zsends = []

    def piece(p, k):
        return zbuf.at[p, pl.ds(k * CH, CH)]

    def zsend(src, p, k, dcol):
        n = len(zsends)
        c = pltpu.make_async_remote_copy(
            src_ref=src, dst_ref=piece(p, k), send_sem=zs.at[n], recv_sem=zr.at[p, k],
            device_id=(row, dcol), device_id_type=MESH,
        )
        c.start()
        zsends.append(c)

    def zwait(p, k):
        pltpu.make_async_copy(piece(p, k), piece(p, k), zr.at[p, k]).wait()

    def own(k):
        return zt.at[pl.ds(k * CH, CH)]

    cp, cm, c2 = zh * 4 + yp, zh * 4 + ym, zh * 4 + y2
    q, qp, qm, q2 = oh * 4 + y, oh * 4 + yp, oh * 4 + ym, oh * 4 + y2

    def send_z(ks):
        for k in ks:
            zsend(own(k), col, k, q)

    def send_own():
        for k in range(NCH):
            zsend(own(k), col, k, cp)
            zsend(own(k), col, k, cm)

    def forward_own(ks):
        for k in ks:
            if k % 2 == 0:
                zwait(cm, k)
                zsend(piece(cm, k), cm, k, cp)
            else:
                zwait(cp, k)
                zsend(piece(cp, k), cp, k, cm)

    def send_far(ks):
        for k in ks:
            zwait(q, k)
            zsend(piece(q, k), q, k, cp)
            zsend(piece(q, k), q, k, cm)

    def forward_far(ks):
        for k in ks:
            if k % 2 == 0:
                zwait(qm, k)
                zsend(piece(qm, k), qm, k, cp)
            else:
                zwait(qp, k)
                zsend(piece(qp, k), qp, k, cm)

    send_z(range(FIRST_Z))
    send_own()

    sel = sel_ref[...]
    hot = (lax.broadcasted_iota(jnp.int32, (128, 128), 0) == sel % 128).astype(F32)
    rows_hot = lax.broadcasted_iota(jnp.int32, (32, 128), 0) == sel // 128

    def lookup(table):
        got = jnp.dot(table, hot, precision=lax.Precision.HIGHEST, preferred_element_type=F32)
        return jnp.sum(jnp.where(rows_hot, got, 0.0), axis=0, keepdims=True)

    shifts[0:1] = lookup(alpha_ref[...])
    shifts[1:2] = lookup(beta_ref[...])
    alpha = shifts[0:1]
    beta = shifts[1:2]

    slots = [slot_ref[0:1, 63:64], slot_ref[0:1, 62:63]]

    def half(ref, w, lanes):
        odd = jnp.broadcast_to(slots[w] % 2 == 1, (BLK, lanes.stop - lanes.start))
        return jnp.where(odd, ref[BLK:, lanes], ref[:BLK, lanes])

    def pick(ref, w, which, count):
        got = ref[w, 0]
        for i in range(1, count):
            got = jnp.where(jnp.broadcast_to(which == i, (SUB, 128)), ref[w, i], got)
        return got

    def prepare(w):
        cols = slice(BLK, 2 * BLK) if w == 0 else slice(0, BLK)
        s_diag = half(s_ref, w, cols)
        t_diag = half(t_ref, w, cols)
        sd[...] = s_diag
        td[...] = t_diag
        s_hi, s_lo = split(s_diag)
        t_hi, t_lo = split(t_diag)
        for g in range(2):
            c = slice(g * 128, g * 128 + 128)
            lmat[g, 0:256, 0:128] = s_hi[:, c]
            lmat[g, 0:256, 128:256] = t_hi[:, c]
            lmat[g, 256:512, 0:128] = s_lo[:, c]
            lmat[g, 256:512, 128:256] = t_lo[:, c]
        rbuf[...] = half(side_ref, w, slice(0, 128))

    lane = lax.broadcasted_iota(jnp.int32, (SUB, 128), 1)
    subl = lax.broadcasted_iota(jnp.int32, (SUB, 128), 0)

    def solve(w):
        xpad[...] = jnp.zeros_like(xpad)

        def panel(t, _):
            p = PANELS - 1 - t
            r0 = pl.multiple_of(p * SUB, SUB)
            g = p // 4
            off = pl.multiple_of((p % 4) * SUB, SUB)
            lanes = pl.ds(pl.multiple_of(g * 128, 128), 128)
            turn = (128 - off) % 128
            s_rows = pltpu.roll(sd[pl.ds(r0, SUB), lanes], turn, 1)
            t_rows = pltpu.roll(td[pl.ds(r0, SUB), lanes], turn, 1)
            on_diag = lane == subl
            s_d = jnp.sum(jnp.where(on_diag, s_rows, 0.0), axis=1, keepdims=True)
            t_d = jnp.sum(jnp.where(on_diag, t_rows, 0.0), axis=1, keepdims=True)
            inv = 1.0 / (beta * s_d - alpha * t_d)
            for j in range(1, SUB):
                h = 8 * (j // 8 + 1)
                c_j = beta * s_rows[0:h, j:j + 1] - alpha * t_rows[0:h, j:j + 1]
                coef[j, 0:h] = jnp.where(subl[0:h] < j, c_j * inv[j:j + 1], 0.0)
            r = [rbuf[pl.ds(r0 + 8 * i, 8), :] for i in range(4)]
            for j in reversed(range(1, SUB)):
                i = j // 8
                entry = jnp.broadcast_to(r[i][j % 8:j % 8 + 1], (8, 128))
                for a in range(i + 1):
                    r[a] = r[a] - coef[j, 8 * a:8 * a + 8] * entry
            x_p = jnp.concatenate(r, 0) * inv
            cand[w, pl.ds(r0, SUB)] = x_p

            @pl.when(p != pi)
            def _():
                stage1(w, p).start()

            @pl.when(p == pi)
            def _():
                st1[w, pi] = x_p

            xpad[pl.ds(off, SUB)] = beta * x_p
            xpad[pl.ds(128 + off, SUB)] = -(alpha * x_p)
            hi, lo = split(xpad[...])
            prod = dot(lmat[g], jnp.concatenate([hi, lo], 1))
            rbuf[...] -= prod[0:256, 0:128] + (prod[0:256, 128:256] + prod[256:512, 0:128])
            xpad[pl.ds(off, SUB)] = jnp.zeros((SUB, 128), F32)
            xpad[pl.ds(128 + off, SUB)] = jnp.zeros((SUB, 128), F32)
            return 0

        lax.fori_loop(0, PANELS, panel, 0)

    def stage1(w, p):
        return pltpu.make_async_remote_copy(
            src_ref=cand.at[w, pl.ds(pl.multiple_of(p * SUB, SUB), SUB)], dst_ref=st1.at[w, pi],
            send_sem=s1s.at[w, p], recv_sem=s1r.at[w, pi],
            device_id=(zlo * 8 + p, col), device_id_type=MESH,
        )

    def stage2(w):
        owner = slots[w] // 2
        for d in range(1, 8):
            src = (pi + d) % 8
            pltpu.make_async_copy(st1.at[w, src], st1.at[w, src], s1r.at[w, src]).wait()
        st2[w, zlo] = pick(st1, w, owner % 8, 8)
        for d in range(1, 4):
            pltpu.make_async_remote_copy(
                src_ref=st2.at[w, zlo], dst_ref=st2.at[w, zlo],
                send_sem=s2s.at[w, d], recv_sem=s2r.at[w, zlo],
                device_id=(((zlo + d) % 4) * 8 + pi, col), device_id_type=MESH,
            ).start()

    def mine():
        return pl.ds(pl.multiple_of(pi * SUB, SUB), SUB)

    def stage3(w):
        owner = slots[w] // 2
        for d in range(1, 4):
            src = (zlo + d) % 4
            pltpu.make_async_copy(st2.at[w, src], st2.at[w, src], s2r.at[w, src]).wait()
        xw[w, mine()] = pick(st2, w, owner // 8, 4)
        for d in range(1, 8):
            pltpu.make_async_remote_copy(
                src_ref=xw.at[w, mine()], dst_ref=xw.at[w, mine()],
                send_sem=s3s.at[w, d], recv_sem=s3r.at[w, pi],
                device_id=(zlo * 8 + (pi + d) % 8, col), device_id_type=MESH,
            ).start()

    def stage4(w):
        for d in range(1, 8):
            src = (pi + d) % 8
            part = xw.at[w, pl.ds(pl.multiple_of(src * SUB, SUB), SUB)]
            pltpu.make_async_copy(part, part, s3r.at[w, src]).wait()

    def drain(w):
        for d in range(1, 8):
            p = (pi + d) % 8
            stage1(w, p).wait_send()
            pltpu.make_async_copy(xw.at[w, mine()], xw.at[w, mine()], s3s.at[w, d]).wait()
        for d in range(1, 4):
            pltpu.make_async_copy(st2.at[w, zlo], st2.at[w, zlo], s2s.at[w, d]).wait()

    def apply(s_cols, t_cols, x):
        return dot3(s_cols, beta * x) - dot3(t_cols, alpha * x)

    for c in loads[:3]:
        c.wait()
    prepare(0)
    solve(0)
    stage2(0)
    send_z(range(FIRST_Z, NCH))
    forward_own(range(NCH))
    prepare(1)
    stage3(0)
    send_far(range(FIRST_Z))
    stage4(0)

    right = slice(BLK, 2 * BLK)
    rbuf[...] -= apply(half(s_ref, 1, right), half(t_ref, 1, right), xw[0])
    solve(1)
    stage2(1)
    send_far(range(FIRST_Z, NCH))
    for h in range(2):
        rs = slice(h * BLK, h * BLK + BLK)
        out_side[rs, :] = side_ref[rs, :] - apply(s_ref[rs, BLK:], t_ref[rs, BLK:], xw[0])
    stage3(1)
    forward_far(range(NCH))
    stage4(1)

    for h in range(2):
        rs = slice(h * BLK, h * BLK + BLK)
        new = out_side[rs, :] - apply(s_ref[rs, :BLK], t_ref[rs, :BLK], xw[1])
        here = row * 2 + h
        new = jnp.where(jnp.broadcast_to(slots[1] == here, (BLK, 128)), xw[1], new)
        out_side[rs, :] = jnp.where(jnp.broadcast_to(slots[0] == here, (BLK, 128)), xw[0], new)

    loads[3].wait()

    def product(c, first):
        at = pl.ds(pl.multiple_of(c * SUB, SUB), SUB)
        x = jnp.concatenate([xw[1, at], xw[0, at]], 0)
        xh, xl = split(x)
        xs = jnp.concatenate([xh, xl, xh], 0)

        def chunk(m, _):
            rows = pl.ds(pl.multiple_of(m * 256, 256), 256)
            zh_, zl_ = split(zbuf[c, :, rows])
            zz = jnp.concatenate([zh_, zh_, zl_], 0)
            part = lax.dot_general(zz, xs, (((0,), (0,)), ((), ())), preferred_element_type=F32)
            out_vec[rows, :] = part if first else out_vec[rows, :] + part
            return 0

        lax.fori_loop(0, ORD // 256, chunk, 0)

    product(col, True)
    for k in range(NCH):
        zwait(cp if k % 2 == 0 else cm, k)
    product(cp, False)
    product(cm, False)
    for k in range(NCH):
        zwait(c2, k)
    product(c2, False)
    product(q, False)
    for k in range(NCH):
        zwait(qp if k % 2 == 0 else qm, k)
    product(qp, False)
    product(qm, False)
    for k in range(NCH):
        zwait(q2, k)
    product(q2, False)
    for c in zsends:
        c.wait_send()
    drain(0)
    drain(1)


def on_device(right_sides, pencil_s, pencil_t, value_alpha, value_beta, selected, block_slot, right_basis, vectors):
    zt = right_basis.transpose(1, 2, 0).reshape(64, ORD)
    vm = pl.BlockSpec(memory_space=pltpu.VMEM)
    dma = pltpu.SemaphoreType.DMA
    sides, prod = pl.pallas_call(
        kernel,
        out_shape=(jax.ShapeDtypeStruct((512, 128), F32), jax.ShapeDtypeStruct((ORD, 128), F32)),
        in_specs=[vm] * 4 + [pl.BlockSpec(memory_space=pl.ANY)] * 4,
        out_specs=(vm, vm),
        scratch_shapes=[
            pltpu.VMEM((512, 128), F32),
            pltpu.VMEM((512, 512), F32),
            pltpu.VMEM((512, 512), F32),
            pltpu.VMEM((8, 64, ORD), F32),
            pltpu.VMEM((BLK, BLK), F32),
            pltpu.VMEM((BLK, BLK), F32),
            pltpu.VMEM((2, 512, 256), BF),
            pltpu.VMEM((BLK, 128), F32),
            pltpu.VMEM((2, BLK, 128), F32),
            pltpu.VMEM((2, 8, SUB, 128), F32),
            pltpu.VMEM((2, 4, SUB, 128), F32),
            pltpu.VMEM((2, BLK, 128), F32),
            pltpu.VMEM((256, 128), F32),
            pltpu.VMEM((SUB, SUB, 128), F32),
            pltpu.VMEM((8, 128), F32),
            dma((8, NCH)), dma((7 * NCH,)),
            dma((2, 8)), dma((2, 8)), dma((2, 4)), dma((2, 4)), dma((2, 8)), dma((2, 8)),
            dma((4,)),
        ],
        compiler_params=pltpu.CompilerParams(
            collective_id=0, has_side_effects=True, vmem_limit_bytes=60 << 20
        ),
    )(
        block_slot.reshape(1, 64), value_alpha.reshape(32, 128), value_beta.reshape(32, 128),
        selected.reshape(1, 128), right_sides, pencil_s, pencil_t, zt,
    )
    return sides, vectors + prod


def solution(mesh):
    return jax.shard_map(
        on_device,
        mesh=mesh,
        in_specs=(
            P("row", "col"), P("row", None), P("row", None), P(), P(), P("col"), P(),
            P("row", None, "col"), P("row", "col"),
        ),
        out_specs=(P("row", "col"), P("row", "col")),
        check_vma=False,
    )
```

time: 970 us -> 82.4 us (0.08)
  waiting for transfers between devices: 842 us -> 0 us
  Pallas kernels: 0 us -> 77.3 us
  matrix products: 37.3 us -> 0 us
  between operations: 19.3 us -> 0.67 us
  local copies, waits for them, and re-layouts: 18.7 us -> 0.71 us
  blocking collectives: 16.7 us -> 0 us
  other arithmetic: 18.7 us -> 2.34 us
    psum x2 -> x0, waiting for transfers between devices: 502 us -> none  [from_root(): return lax.psum(block, axis)]
    reduce_scatter x2 -> x0, waiting for transfers between devices: 331 us -> none  [block_term(): lax.psum_scatter(partial_value, 'col', scatter_dimension=1, tiled=True)]
    pallas_call x0 -> x1, Pallas kernels: none -> 77.3 us  [on_device(): pl.pallas_call(kernel, out_shape=(jax.ShapeDtypeStruct((512, 128), F32),...]
    dot_general x38 -> x0, matrix products: 37.3 us -> none  [the longest x2 18.1 us: block_term(): jnp.dot(basis_cols, matched_rows, precision=exact_mode, preferred_element...]
    all_to_all x1 -> x0, blocking collectives: 16.7 us -> none  [block_term(): lax.all_to_all(solved, 'col', split_axis=0, concat_axis=1, tiled=True)]
  transfers between devices with their start and end apart: 5 -> 0, of which waited for: 5 -> 0; matrix products, arithmetic and copies ran while one was open for 3% -> 0% of each run, Pallas kernels for 0% -> 0%
where the time goes in v1:
time: 82.4 us; the launch traced here: 81 us
  Pallas kernels  77.3 us (94%)
  other arithmetic  2.34 us (3%)
    pallas_call x1, Pallas kernels, on_device(): pl.pallas_call(kernel, out_shape=(jax.ShapeDtypeStruct((512, 128), F32),...  77.3 us
    add x1, other arithmetic, on_device(): return (sides, vectors + prod)  2.34 us

profile of v1, /device:TPU:1, one launch (start us, length us, event | category | flops | bytes accessed | tf_op | source)
XLA Modules:
  0.0 81.0 jit_solution(5097855704689419969)
XLA Ops:
  0.6 0.0 copy-start
  0.6 77.3 %shard_map.104 = (f32[512,128]{1,0:T(8,128)}, f32[2048,128]{1,0:T(8,128)}) custom-call(s32[1,64]{1,0:T(1,128)} %bitcast.10, f32[32,128]{1,0:T(8,128)} %bitcast.8, f32[32,128]{1,0:T(8,128)} %bitcast.9, s32[1,128]{1,0:T(1,128)} %bitcast.11, f32[512,128]{1,0:T(8,128)} %side_hbm.1, f32[512,512]{1,0:T(8,128)} %s_hbm.1, f32[512,512]{1,0:T(8,128)} %t_hbm.1, ...), custom_call_target="tpu_custom_call" | custom-call | tf_op jit(solution)/shard_map/pallas_call | solution.py:344
  77.9 0.0 copy-done
  77.9 0.0 copy-start.1
  78.0 2.3 %add.3 = f32[2048,128]{1,0:T(8,128)} add(f32[2048,128]{1,0:T(8,128)S(1)} %copy-done, f32[2048,128]{1,0:T(8,128)} %get-tuple-element.5) | non-fusion elementwise | flops 262144 | bytes 3145728 | tf_op jit(solution)/shard_map/add | solution.py:376
  80.3 0.0 copy-done.1
  80.3 0.7 copy.12
Async XLA Ops:
  0.6 77.3 %copy-start = (f32[2048,128]{1,0:T(8,128)S(1)}, f32[2048,128]{1,0:T(8,128)}, u32[]{:S(2)}) copy-start(f32[2048,128]{1,0:T(8,128)} %param.17) | copy-start | bytes 3145732
  77.9 2.4 %copy-start.1 = (f32[512,128]{1,0:T(8,128)S(1)}, f32[512,128]{1,0:T(8,128)}, u32[]{:S(2)}) copy-start(f32[512,128]{1,0:T(8,128)} %get-tuple-element.8) | copy-start | bytes 786436

commit v2 on v1

--- a/solution.py
+++ b/solution.py
@@ -16,7 +16,8 @@
 ORD = 2048
 F32 = jnp.float32
 BF = jnp.bfloat16
-FIRST_Z = 3
+Z_A = 2
+Z_B = 6
 
 
 def split(v):
@@ -28,16 +29,10 @@
     return jnp.dot(a, b, preferred_element_type=F32)
 
 
-def dot3(a, b):
-    ah, al = split(a)
-    bh, bl = split(b)
-    return dot(ah, bh) + (dot(ah, bl) + dot(al, bh))
-
-
 def kernel(
     slot_ref, alpha_ref, beta_ref, sel_ref, side_hbm, s_hbm, t_hbm, zt,
     out_side, out_vec,
-    side_ref, s_ref, t_ref, zbuf, sd, td, lmat, rbuf, cand, st1, st2, xw, xpad, coef, shifts,
+    side_ref, s_ref, t_ref, zbuf, zhi, zlow, sd, td, lmat, rbuf, cand, st1, st2, xw, xpad, coef, shifts,
     zr, zs, s1r, s1s, s2r, s2s, s3r, s3s, lsem,
 ):
     row = lax.axis_index("row")
@@ -74,7 +69,7 @@
             device_id=(row, dcol), device_id_type=MESH,
         )
         c.start()
-        zsends.append(c)
+        zsends.append((p, k))
 
     def zwait(p, k):
         pltpu.make_async_copy(piece(p, k), piece(p, k), zr.at[p, k]).wait()
@@ -118,7 +113,7 @@
                 zwait(qp, k)
                 zsend(piece(qp, k), qp, k, cm)
 
-    send_z(range(FIRST_Z))
+    send_z(range(Z_A))
     send_own()
 
     sel = sel_ref[...]
@@ -165,10 +160,12 @@
     lane = lax.broadcasted_iota(jnp.int32, (SUB, 128), 1)
     subl = lax.broadcasted_iota(jnp.int32, (SUB, 128), 0)
 
-    def solve(w):
+    def solve(w, hooks):
         xpad[...] = jnp.zeros_like(xpad)
 
         def panel(t, _):
+            for at, hook in hooks.items():
+                pl.when(t == at)(hook)
             p = PANELS - 1 - t
             r0 = pl.multiple_of(p * SUB, SUB)
             g = p // 4
@@ -264,31 +261,80 @@
             pltpu.make_async_copy(st2.at[w, zlo], st2.at[w, zlo], s2s.at[w, d]).wait()
 
     def apply(s_cols, t_cols, x):
-        return dot3(s_cols, beta * x) - dot3(t_cols, alpha * x)
-
+        lh, ll = split(jnp.concatenate([s_cols, t_cols], 1))
+        rh, rl = split(jnp.concatenate([beta * x, -(alpha * x)], 0))
+        wide = dot(lh, jnp.concatenate([rh, rl], 1))
+        return wide[:, 0:128] + (wide[:, 128:256] + dot(ll, rh))
+
+    order = [col, cp, cm, c2, q, qp, qm, q2]
+
+    def convert(pair):
+        first, second = order[2 * pair], order[2 * pair + 1]
+
+        def chunk(m, _):
+            rows = pl.ds(pl.multiple_of(m * 256, 256), 256)
+            both = jnp.concatenate([zbuf[first, :, rows], zbuf[second, :, rows]], 0)
+            hi, lo = split(both.T)
+            zhi[rows, 128 * pair:128 * pair + 128] = hi
+            zlow[rows, 128 * pair:128 * pair + 128] = lo
+            return 0
+
+        lax.fori_loop(0, ORD // 256, chunk, 0)
+
+    def product(pairs, first):
+        xs = []
+        for c in order[2 * pairs[0]:2 * pairs[-1] + 2]:
+            at = pl.ds(pl.multiple_of(c * SUB, SUB), SUB)
+            xs += [xw[1, at], xw[0, at]]
+        xh, xl = split(jnp.concatenate(xs, 0))
+        wide_x = jnp.concatenate([xh, xl], 1)
+        ks = slice(128 * pairs[0], 128 * pairs[-1] + 128)
+
+        def chunk(m, _):
+            rows = pl.ds(pl.multiple_of(m * 256, 256), 256)
+            wide = dot(zhi[rows, ks], wide_x)
+            part = wide[:, 0:128] + (wide[:, 128:256] + dot(zlow[rows, ks], xh))
+            out_vec[rows, :] = part if first else out_vec[rows, :] + part
+            return 0
+
+        lax.fori_loop(0, ORD // 256, chunk, 0)
+
+    right = slice(BLK, 2 * BLK)
     for c in loads[:3]:
         c.wait()
     prepare(0)
-    solve(0)
+    solve(0, {})
     stage2(0)
-    send_z(range(FIRST_Z, NCH))
-    forward_own(range(NCH))
+    forward_own(range(0, 4))
     prepare(1)
     stage3(0)
-    send_far(range(FIRST_Z))
+    send_z(range(Z_A, Z_B))
+    send_far(range(Z_A))
     stage4(0)
-
-    right = slice(BLK, 2 * BLK)
     rbuf[...] -= apply(half(s_ref, 1, right), half(t_ref, 1, right), xw[0])
-    solve(1)
+    hooks = {0: lambda: forward_own([4, 5]), 2: lambda: forward_own([6, 7])}
+    hooks[5] = lambda: send_far([Z_A])
+    solve(1, hooks)
     stage2(1)
-    send_far(range(FIRST_Z, NCH))
+    send_far(range(Z_A + 1, Z_B))
+    forward_far(range(0, Z_A))
     for h in range(2):
         rs = slice(h * BLK, h * BLK + BLK)
         out_side[rs, :] = side_ref[rs, :] - apply(s_ref[rs, BLK:], t_ref[rs, BLK:], xw[0])
+    loads[3].wait()
     stage3(1)
-    forward_far(range(NCH))
+    send_z(range(Z_B, NCH))
+    for k in range(NCH):
+        zwait(cp if k % 2 == 0 else cm, k)
+    convert(0)
+    forward_far(range(Z_A, Z_B - 1))
+    for k in range(NCH):
+        zwait(c2, k)
+    convert(1)
+    forward_far(range(Z_B - 1, Z_B))
     stage4(1)
+    send_far(range(Z_B, NCH))
+    product([0, 1], True)
 
     for h in range(2):
         rs = slice(h * BLK, h * BLK + BLK)
@@ -297,42 +343,17 @@
         new = jnp.where(jnp.broadcast_to(slots[1] == here, (BLK, 128)), xw[1], new)
         out_side[rs, :] = jnp.where(jnp.broadcast_to(slots[0] == here, (BLK, 128)), xw[0], new)
 
-    loads[3].wait()
-
-    def product(c, first):
-        at = pl.ds(pl.multiple_of(c * SUB, SUB), SUB)
-        x = jnp.concatenate([xw[1, at], xw[0, at]], 0)
-        xh, xl = split(x)
-        xs = jnp.concatenate([xh, xl, xh], 0)
-
-        def chunk(m, _):
-            rows = pl.ds(pl.multiple_of(m * 256, 256), 256)
-            zh_, zl_ = split(zbuf[c, :, rows])
-            zz = jnp.concatenate([zh_, zh_, zl_], 0)
-            part = lax.dot_general(zz, xs, (((0,), (0,)), ((), ())), preferred_element_type=F32)
-            out_vec[rows, :] = part if first else out_vec[rows, :] + part
-            return 0
-
-        lax.fori_loop(0, ORD // 256, chunk, 0)
-
-    product(col, True)
-    for k in range(NCH):
-        zwait(cp if k % 2 == 0 else cm, k)
-    product(cp, False)
-    product(cm, False)
-    for k in range(NCH):
-        zwait(c2, k)
-    product(c2, False)
-    product(q, False)
+    forward_far(range(Z_B, NCH))
     for k in range(NCH):
         zwait(qp if k % 2 == 0 else qm, k)
-    product(qp, False)
-    product(qm, False)
+    convert(2)
+    product([2], False)
     for k in range(NCH):
         zwait(q2, k)
-    product(q2, False)
-    for c in zsends:
-        c.wait_send()
+    convert(3)
+    product([3], False)
+    for n, (p, k) in enumerate(zsends):
+        pltpu.make_async_copy(piece(p, k), piece(p, k), zs.at[n]).wait()
     drain(0)
     drain(1)
 
@@ -344,13 +365,15 @@
     sides, prod = pl.pallas_call(
         kernel,
         out_shape=(jax.ShapeDtypeStruct((512, 128), F32), jax.ShapeDtypeStruct((ORD, 128), F32)),
-        in_specs=[vm] * 4 + [pl.BlockSpec(memory_space=pl.ANY)] * 4,
+        in_specs=[vm] * 4 + [pl.BlockSpec(memory_space=pltpu.HBM)] * 4,
         out_specs=(vm, vm),
         scratch_shapes=[
             pltpu.VMEM((512, 128), F32),
             pltpu.VMEM((512, 512), F32),
             pltpu.VMEM((512, 512), F32),
             pltpu.VMEM((8, 64, ORD), F32),
+            pltpu.VMEM((ORD, 512), BF),
+            pltpu.VMEM((ORD, 512), BF),
             pltpu.VMEM((BLK, BLK), F32),
             pltpu.VMEM((BLK, BLK), F32),
             pltpu.VMEM((2, 512, 256), BF),

time: 82.4 us -> 64.1 us (0.78)
  the two profiles are of different devices: /device:TPU:1 before, /device:TPU:8 now
where the time goes in v2:
time: 64.1 us; the launch traced here: 63.9 us
  Pallas kernels  60.2 us (94%)
  other arithmetic  2.34 us (4%)
  local copies, waits for them, and re-layouts  0.71 us (1%)
  between operations  0.67 us (1%)
    pallas_call x1, Pallas kernels, on_device(): pl.pallas_call(kernel, out_shape=(jax.ShapeDtypeStruct((512, 128), F32),...  60.2 us
    add x1, other arithmetic, on_device(): return (sides, vectors + prod)  2.34 us

profile of v2, /device:TPU:8, one launch (start us, length us, event | category | flops | bytes accessed | tf_op | source)
XLA Modules:
  0.0 63.9 jit_solution(1698207970089064324)
XLA Ops:
  0.6 0.0 copy-start
  0.6 60.2 %shard_map.104 = (f32[512,128]{1,0:T(8,128)}, f32[2048,128]{1,0:T(8,128)}) custom-call(s32[1,64]{1,0:T(1,128)} %bitcast.10, f32[32,128]{1,0:T(8,128)} %bitcast.8, f32[32,128]{1,0:T(8,128)} %bitcast.9, s32[1,128]{1,0:T(1,128)} %bitcast.11, f32[512,128]{1,0:T(8,128)} %side_hbm.1, f32[512,512]{1,0:T(8,128)} %s_hbm.1, f32[512,512]{1,0:T(8,128)} %t_hbm.1, ...), custom_call_target="tpu_custom_call" | custom-call | tf_op jit(solution)/shard_map/pallas_call | solution.py:365
  60.9 0.0 copy-done
  60.9 0.0 copy-start.1
  60.9 2.3 %add.3 = f32[2048,128]{1,0:T(8,128)} add(f32[2048,128]{1,0:T(8,128)S(1)} %copy-done, f32[2048,128]{1,0:T(8,128)} %get-tuple-element.5) | non-fusion elementwise | flops 262144 | bytes 3145728 | tf_op jit(solution)/shard_map/add | solution.py:399
  63.2 0.0 copy-done.1
  63.2 0.7 %copy.12 = f32[512,128]{1,0:T(8,128)} copy(f32[512,128]{1,0:T(8,128)S(1)} %copy-done.1) | data formatting | bytes 524288
Async XLA Ops:
  0.6 60.2 %copy-start = (f32[2048,128]{1,0:T(8,128)S(1)}, f32[2048,128]{1,0:T(8,128)}, u32[]{:S(2)}) copy-start(f32[2048,128]{1,0:T(8,128)} %param.17) | copy-start | bytes 3145732
  60.9 2.4 %copy-start.1 = (f32[512,128]{1,0:T(8,128)S(1)}, f32[512,128]{1,0:T(8,128)}, u32[]{:S(2)}) copy-start(f32[512,128]{1,0:T(8,128)} %get-tuple-element.8) | copy-start | bytes 786436

commit v3 on v2

--- a/solution.py
+++ b/solution.py
@@ -12,12 +12,11 @@
 SUB = 32
 PANELS = BLK // SUB
 NCH = 8
-CH = 64 // NCH
 ORD = 2048
+CH = ORD // NCH
 F32 = jnp.float32
 BF = jnp.bfloat16
-Z_A = 2
-Z_B = 6
+Z_A = 3
 
 
 def split(v):
@@ -32,7 +31,7 @@
 def kernel(
     slot_ref, alpha_ref, beta_ref, sel_ref, side_hbm, s_hbm, t_hbm, zt,
     out_side, out_vec,
-    side_ref, s_ref, t_ref, zbuf, zhi, zlow, sd, td, lmat, rbuf, cand, st1, st2, xw, xpad, coef, shifts,
+    side_ref, s_ref, t_ref, zbuf, zhi, zlow, xcat, sd, td, lmat, rbuf, cand, st1, st2, xw, xpad, coef, shifts,
     zr, zs, s1r, s1s, s2r, s2s, s3r, s3s, lsem,
 ):
     row = lax.axis_index("row")
@@ -55,12 +54,11 @@
     peers += [(((zlo + d) % 4) * 8 + pi, col) for d in range(1, 4)]
     for d in peers:
         pl.semaphore_signal(bar, inc=1, device_id=d, device_id_type=MESH)
-    pl.semaphore_wait(bar, len(peers))
 
     zsends = []
 
     def piece(p, k):
-        return zbuf.at[p, pl.ds(k * CH, CH)]
+        return zbuf.at[p, :, pl.ds(k * CH, CH)]
 
     def zsend(src, p, k, dcol):
         n = len(zsends)
@@ -75,7 +73,7 @@
         pltpu.make_async_copy(piece(p, k), piece(p, k), zr.at[p, k]).wait()
 
     def own(k):
-        return zt.at[pl.ds(k * CH, CH)]
+        return zt.at[:, pl.ds(k * CH, CH)]
 
     cp, cm, c2 = zh * 4 + yp, zh * 4 + ym, zh * 4 + y2
     q, qp, qm, q2 = oh * 4 + y, oh * 4 + yp, oh * 4 + ym, oh * 4 + y2
@@ -113,8 +111,6 @@
                 zwait(qp, k)
                 zsend(piece(qp, k), qp, k, cm)
 
-    send_z(range(Z_A))
-    send_own()
 
     sel = sel_ref[...]
     hot = (lax.broadcasted_iota(jnp.int32, (128, 128), 0) == sel % 128).astype(F32)
@@ -160,55 +156,62 @@
     lane = lax.broadcasted_iota(jnp.int32, (SUB, 128), 1)
     subl = lax.broadcasted_iota(jnp.int32, (SUB, 128), 0)
 
+    def coefficients(p, b):
+        r0 = pl.multiple_of(p * SUB, SUB)
+        lanes = pl.ds(pl.multiple_of((p // 4) * 128, 128), 128)
+        turn = (128 - (p % 4) * SUB) % 128
+        s_rows = pltpu.roll(sd[pl.ds(r0, SUB), lanes], turn, 1)
+        t_rows = pltpu.roll(td[pl.ds(r0, SUB), lanes], turn, 1)
+        on_diag = lane == subl
+        s_d = jnp.sum(jnp.where(on_diag, s_rows, 0.0), axis=1, keepdims=True)
+        t_d = jnp.sum(jnp.where(on_diag, t_rows, 0.0), axis=1, keepdims=True)
+        inv = 1.0 / (beta * s_d - alpha * t_d)
+        for j in range(1, SUB):
+            h = 8 * (j // 8 + 1)
+            c_j = beta * s_rows[0:h, j:j + 1] - alpha * t_rows[0:h, j:j + 1]
+            coef[b, j, 0:h] = jnp.where(subl[0:h] < j, c_j * inv[j:j + 1], 0.0)
+        coef[b, 0] = inv
+
     def solve(w, hooks):
         xpad[...] = jnp.zeros_like(xpad)
 
-        def panel(t, _):
-            for at, hook in hooks.items():
-                pl.when(t == at)(hook)
-            p = PANELS - 1 - t
-            r0 = pl.multiple_of(p * SUB, SUB)
-            g = p // 4
-            off = pl.multiple_of((p % 4) * SUB, SUB)
-            lanes = pl.ds(pl.multiple_of(g * 128, 128), 128)
-            turn = (128 - off) % 128
-            s_rows = pltpu.roll(sd[pl.ds(r0, SUB), lanes], turn, 1)
-            t_rows = pltpu.roll(td[pl.ds(r0, SUB), lanes], turn, 1)
-            on_diag = lane == subl
-            s_d = jnp.sum(jnp.where(on_diag, s_rows, 0.0), axis=1, keepdims=True)
-            t_d = jnp.sum(jnp.where(on_diag, t_rows, 0.0), axis=1, keepdims=True)
-            inv = 1.0 / (beta * s_d - alpha * t_d)
-            for j in range(1, SUB):
-                h = 8 * (j // 8 + 1)
-                c_j = beta * s_rows[0:h, j:j + 1] - alpha * t_rows[0:h, j:j + 1]
-                coef[j, 0:h] = jnp.where(subl[0:h] < j, c_j * inv[j:j + 1], 0.0)
-            r = [rbuf[pl.ds(r0 + 8 * i, 8), :] for i in range(4)]
-            for j in reversed(range(1, SUB)):
-                i = j // 8
-                entry = jnp.broadcast_to(r[i][j % 8:j % 8 + 1], (8, 128))
-                for a in range(i + 1):
-                    r[a] = r[a] - coef[j, 8 * a:8 * a + 8] * entry
-            x_p = jnp.concatenate(r, 0) * inv
-            cand[w, pl.ds(r0, SUB)] = x_p
-
-            @pl.when(p != pi)
-            def _():
-                stage1(w, p).start()
-
-            @pl.when(p == pi)
-            def _():
-                st1[w, pi] = x_p
-
-            xpad[pl.ds(off, SUB)] = beta * x_p
-            xpad[pl.ds(128 + off, SUB)] = -(alpha * x_p)
-            hi, lo = split(xpad[...])
-            prod = dot(lmat[g], jnp.concatenate([hi, lo], 1))
-            rbuf[...] -= prod[0:256, 0:128] + (prod[0:256, 128:256] + prod[256:512, 0:128])
-            xpad[pl.ds(off, SUB)] = jnp.zeros((SUB, 128), F32)
-            xpad[pl.ds(128 + off, SUB)] = jnp.zeros((SUB, 128), F32)
+        def pair(t2, _):
+            for b in range(2):
+                t = 2 * t2 + b
+                p = PANELS - 1 - t
+                for at, hook in hooks.items():
+                    if at % 2 == b:
+                        pl.when(t2 == at // 2)(hook)
+                r0 = pl.multiple_of(p * SUB, SUB)
+                off = pl.multiple_of((p % 4) * SUB, SUB)
+                r = [rbuf[pl.ds(r0 + 8 * i, 8), :] for i in range(4)]
+                for j in reversed(range(1, SUB)):
+                    i = j // 8
+                    entry = jnp.broadcast_to(r[i][j % 8:j % 8 + 1], (8, 128))
+                    for a in range(i + 1):
+                        r[a] = r[a] - coef[b, j, 8 * a:8 * a + 8] * entry
+                x_p = jnp.concatenate(r, 0) * coef[b, 0]
+                cand[w, pl.ds(r0, SUB)] = x_p
+
+                @pl.when(p != pi)
+                def _():
+                    stage1(w, p).start()
+
+                @pl.when(p == pi)
+                def _():
+                    st1[w, pi] = cand[w, pl.ds(r0, SUB)]
+
+                xpad[pl.ds(off, SUB)] = beta * x_p
+                xpad[pl.ds(128 + off, SUB)] = -(alpha * x_p)
+                hi, lo = split(xpad[...])
+                prod = dot(lmat[p // 4], jnp.concatenate([hi, lo], 1))
+                coefficients(lax.rem(p + PANELS - 1, PANELS), 1 - b)
+                rbuf[...] -= prod[0:256, 0:128] + (prod[0:256, 128:256] + prod[256:512, 0:128])
+                xpad[pl.ds(off, SUB)] = jnp.zeros((SUB, 128), F32)
+                xpad[pl.ds(128 + off, SUB)] = jnp.zeros((SUB, 128), F32)
             return 0
 
-        lax.fori_loop(0, PANELS, panel, 0)
+        lax.fori_loop(0, PANELS // 2, pair, 0)
 
     def stage1(w, p):
         return pltpu.make_async_remote_copy(
@@ -268,74 +271,75 @@
 
     order = [col, cp, cm, c2, q, qp, qm, q2]
 
-    def convert(pair):
+    def convert(pair, m):
         first, second = order[2 * pair], order[2 * pair + 1]
-
+        rows = pl.ds(m * CH, CH)
+        both = jnp.concatenate([zbuf[first, :, rows], zbuf[second, :, rows]], 0)
+        hi, lo = split(both.T)
+        zhi[rows, 128 * pair:128 * pair + 128] = hi
+        zlow[rows, 128 * pair:128 * pair + 128] = lo
+
+    def convert_all(pair):
         def chunk(m, _):
-            rows = pl.ds(pl.multiple_of(m * 256, 256), 256)
-            both = jnp.concatenate([zbuf[first, :, rows], zbuf[second, :, rows]], 0)
-            hi, lo = split(both.T)
-            zhi[rows, 128 * pair:128 * pair + 128] = hi
-            zlow[rows, 128 * pair:128 * pair + 128] = lo
+            convert(pair, m)
             return 0
 
-        lax.fori_loop(0, ORD // 256, chunk, 0)
-
-    def product(pairs, first):
-        xs = []
-        for c in order[2 * pairs[0]:2 * pairs[-1] + 2]:
+        lax.fori_loop(0, NCH, chunk, 0)
+
+    def gather_x():
+        for n, c in enumerate(order):
             at = pl.ds(pl.multiple_of(c * SUB, SUB), SUB)
-            xs += [xw[1, at], xw[0, at]]
-        xh, xl = split(jnp.concatenate(xs, 0))
-        wide_x = jnp.concatenate([xh, xl], 1)
-        ks = slice(128 * pairs[0], 128 * pairs[-1] + 128)
-
-        def chunk(m, _):
-            rows = pl.ds(pl.multiple_of(m * 256, 256), 256)
-            wide = dot(zhi[rows, ks], wide_x)
-            part = wide[:, 0:128] + (wide[:, 128:256] + dot(zlow[rows, ks], xh))
-            out_vec[rows, :] = part if first else out_vec[rows, :] + part
-            return 0
-
-        lax.fori_loop(0, ORD // 256, chunk, 0)
+            for h in range(2):
+                hi, lo = split(xw[1 - h, at])
+                rows = slice(64 * n + SUB * h, 64 * n + SUB * h + SUB)
+                xcat[rows, 0:128] = hi
+                xcat[rows, 128:256] = lo
+
+    def product(m):
+        rows = pl.ds(m * CH, CH)
+        wide = dot(zhi[rows, :], xcat[...])
+        out_vec[rows, :] = wide[:, 0:128] + (wide[:, 128:256] + dot(zlow[rows, :], xcat[:, 0:128]))
 
     right = slice(BLK, 2 * BLK)
     for c in loads[:3]:
         c.wait()
     prepare(0)
+    coefficients(PANELS - 1, 0)
+    pl.semaphore_wait(bar, len(peers))
+    send_z(range(Z_A))
+    send_own()
     solve(0, {})
     stage2(0)
     forward_own(range(0, 4))
     prepare(1)
+    coefficients(PANELS - 1, 0)
     stage3(0)
-    send_z(range(Z_A, Z_B))
+    send_z(range(Z_A, NCH))
+    forward_own(range(4, NCH))
     send_far(range(Z_A))
     stage4(0)
     rbuf[...] -= apply(half(s_ref, 1, right), half(t_ref, 1, right), xw[0])
-    hooks = {0: lambda: forward_own([4, 5]), 2: lambda: forward_own([6, 7])}
-    hooks[5] = lambda: send_far([Z_A])
-    solve(1, hooks)
+    solve(1, {})
     stage2(1)
-    send_far(range(Z_A + 1, Z_B))
-    forward_far(range(0, Z_A))
+    send_far(range(Z_A, Z_A + 2))
     for h in range(2):
         rs = slice(h * BLK, h * BLK + BLK)
         out_side[rs, :] = side_ref[rs, :] - apply(s_ref[rs, BLK:], t_ref[rs, BLK:], xw[0])
     loads[3].wait()
-    stage3(1)
-    send_z(range(Z_B, NCH))
     for k in range(NCH):
         zwait(cp if k % 2 == 0 else cm, k)
-    convert(0)
-    forward_far(range(Z_A, Z_B - 1))
+    convert_all(0)
+    forward_far(range(0, 2))
+    send_far(range(Z_A + 2, Z_A + 3))
     for k in range(NCH):
         zwait(c2, k)
-    convert(1)
-    forward_far(range(Z_B - 1, Z_B))
+    convert_all(1)
+    forward_far(range(2, 3))
+    stage3(1)
+    send_far(range(Z_A + 3, NCH))
+    forward_far(range(3, 5))
     stage4(1)
-    send_far(range(Z_B, NCH))
-    product([0, 1], True)
-
+    gather_x()
     for h in range(2):
         rs = slice(h * BLK, h * BLK + BLK)
         new = out_side[rs, :] - apply(s_ref[rs, :BLK], t_ref[rs, :BLK], xw[1])
@@ -343,15 +347,14 @@
         new = jnp.where(jnp.broadcast_to(slots[1] == here, (BLK, 128)), xw[1], new)
         out_side[rs, :] = jnp.where(jnp.broadcast_to(slots[0] == here, (BLK, 128)), xw[0], new)
 
-    forward_far(range(Z_B, NCH))
     for k in range(NCH):
+        if 5 <= k + 4 < NCH:
+            forward_far([k + 4])
         zwait(qp if k % 2 == 0 else qm, k)
-    convert(2)
-    product([2], False)
-    for k in range(NCH):
         zwait(q2, k)
-    convert(3)
-    product([3], False)
+        convert(2, k)
+        convert(3, k)
+        product(k)
     for n, (p, k) in enumerate(zsends):
         pltpu.make_async_copy(piece(p, k), piece(p, k), zs.at[n]).wait()
     drain(0)
@@ -374,6 +377,7 @@
             pltpu.VMEM((8, 64, ORD), F32),
             pltpu.VMEM((ORD, 512), BF),
             pltpu.VMEM((ORD, 512), BF),
+            pltpu.VMEM((512, 256), BF),
             pltpu.VMEM((BLK, BLK), F32),
             pltpu.VMEM((BLK, BLK), F32),
             pltpu.VMEM((2, 512, 256), BF),
@@ -383,18 +387,20 @@
             pltpu.VMEM((2, 4, SUB, 128), F32),
             pltpu.VMEM((2, BLK, 128), F32),
             pltpu.VMEM((256, 128), F32),
-            pltpu.VMEM((SUB, SUB, 128), F32),
+            pltpu.VMEM((2, SUB, SUB, 128), F32),
             pltpu.VMEM((8, 128), F32),
             dma((8, NCH)), dma((7 * NCH,)),
             dma((2, 8)), dma((2, 8)), dma((2, 4)), dma((2, 4)), dma((2, 8)), dma((2, 8)),
             dma((4,)),
         ],
         compiler_params=pltpu.CompilerParams(
-            collective_id=0, has_side_effects=True, vmem_limit_bytes=60 << 20
+            collective_id=0, has_side_effects=True, vmem_limit_bytes=48 << 20
         ),
     )(
-        block_slot.reshape(1, 64), value_alpha.reshape(32, 128), value_beta.reshape(32, 128),
-        selected.reshape(1, 128), right_sides, pencil_s, pencil_t, zt,
+        *(pltpu.with_memory_space_constraint(v, pltpu.HBM) for v in (
+            block_slot.reshape(1, 64), value_alpha.reshape(32, 128), value_beta.reshape(32, 128),
+            selected.reshape(1, 128), right_sides, pencil_s, pencil_t, zt,
+        )),
     )
     return sides, vectors + prod
 

time: 64.1 us -> 55.6 us (0.87)
  the two profiles are of different devices: /device:TPU:8 before, /device:TPU:1 now
where the time goes in v3:
time: 55.6 us; the launch traced here: 55.4 us
  Pallas kernels  53 us (95%)
  other arithmetic  1.08 us (2%)
  local copies, waits for them, and re-layouts  0.71 us (1%)
  between operations  0.66 us (1%)
    pallas_call x1, Pallas kernels, on_device(): pl.pallas_call(kernel, out_shape=(jax.ShapeDtypeStruct((512, 128), F32),...  53 us

profile of v3, /device:TPU:1, one launch (start us, length us, event | category | flops | bytes accessed | tf_op | source)
XLA Modules:
  0.0 55.4 jit_solution(6398712843228167958)
XLA Ops:
  0.6 0.0 copy-start
  0.6 53.0 %shard_map.104 = (f32[512,128]{1,0:T(8,128)S(1)}, f32[2048,128]{1,0:T(8,128)S(1)}) custom-call(s32[1,64]{1,0:T(1,128)} %bitcast.10, f32[32,128]{1,0:T(8,128)} %bitcast.8, f32[32,128]{1,0:T(8,128)} %bitcast.9, s32[1,128]{1,0:T(1,128)} %bitcast.11, f32[512,128]{1,0:T(8,128)} %side_hbm.1, f32[512,512]{1,0:T(8,128)} %s_hbm.1, f32[512,512]{1,0:T(8,128)} %t_hbm.1, ...), custom_call_target="tpu_custom_call" | custom-call | tf_op jit(solution)/shard_map/pallas_call | solution.py:368
  53.6 0.0 copy-done
  53.7 1.1 %add.3 = f32[2048,128]{1,0:T(8,128)} add(f32[2048,128]{1,0:T(8,128)S(1)} %copy-done, f32[2048,128]{1,0:T(8,128)S(1)} %get-tuple-element.5) | non-fusion elementwise | flops 262144 | bytes 3145728 | tf_op jit(solution)/shard_map/add | solution.py:405
  54.7 0.7 %copy.12 = f32[512,128]{1,0:T(8,128)} copy(f32[512,128]{1,0:T(8,128)S(1)} %get-tuple-element.8) | data formatting | bytes 524288
Async XLA Ops:
  0.6 53.0 %copy-start = (f32[2048,128]{1,0:T(8,128)S(1)}, f32[2048,128]{1,0:T(8,128)}, u32[]{:S(2)}) copy-start(f32[2048,128]{1,0:T(8,128)} %param.17) | copy-start | bytes 3145732

commit v4 on v3

--- a/solution.py
+++ b/solution.py
@@ -29,9 +29,9 @@
 
 
 def kernel(
-    slot_ref, alpha_ref, beta_ref, sel_ref, side_hbm, s_hbm, t_hbm, zt,
+    slot_hbm, alpha_hbm, beta_hbm, sel_hbm, side_hbm, s_hbm, t_hbm, zt,
     out_side, out_vec,
-    side_ref, s_ref, t_ref, zbuf, zhi, zlow, xcat, sd, td, lmat, rbuf, cand, st1, st2, xw, xpad, coef, shifts,
+    slot_ref, alpha_ref, beta_ref, sel_ref, side_ref, s_ref, t_ref, zbuf, zhi, zlow, xcat, sd, td, lmat, rbuf, cand, st1, st2, xw, xpad, coef, shifts,
     zr, zs, s1r, s1s, s2r, s2s, s3r, s3s, lsem,
 ):
     row = lax.axis_index("row")
@@ -43,17 +43,20 @@
     yp, ym, y2 = (y + 1) % 4, (y + 3) % 4, (y + 2) % 4
     oh = 1 - zh
 
-    loads = []
-    for n, (src, dst) in enumerate(((s_hbm, s_ref), (t_hbm, t_ref), (side_hbm, side_ref), (zt, zbuf.at[col]))):
-        loads.append(pltpu.make_async_copy(src, dst, lsem.at[n]))
-        loads[-1].start()
-
     bar = pltpu.get_barrier_semaphore()
     peers = [(row, zh * 4 + yp), (row, zh * 4 + ym), (row, oh * 4 + y)]
     peers += [(zlo * 8 + (pi + d) % 8, col) for d in range(1, 8)]
     peers += [(((zlo + d) % 4) * 8 + pi, col) for d in range(1, 4)]
     for d in peers:
         pl.semaphore_signal(bar, inc=1, device_id=d, device_id_type=MESH)
+
+    loads = []
+    for n, (src, dst) in enumerate((
+        (slot_hbm, slot_ref), (alpha_hbm, alpha_ref), (beta_hbm, beta_ref), (sel_hbm, sel_ref),
+        (s_hbm, s_ref), (t_hbm, t_ref), (side_hbm, side_ref), (zt, zbuf.at[col]),
+    )):
+        loads.append(pltpu.make_async_copy(src, dst, lsem.at[n]))
+        loads[-1].start()
 
     zsends = []
 
@@ -112,6 +115,8 @@
                 zsend(piece(qp, k), qp, k, cm)
 
 
+    for c in loads[:4]:
+        c.wait()
     sel = sel_ref[...]
     hot = (lax.broadcasted_iota(jnp.int32, (128, 128), 0) == sel % 128).astype(F32)
     rows_hot = lax.broadcasted_iota(jnp.int32, (32, 128), 0) == sel // 128
@@ -301,13 +306,13 @@
         out_vec[rows, :] = wide[:, 0:128] + (wide[:, 128:256] + dot(zlow[rows, :], xcat[:, 0:128]))
 
     right = slice(BLK, 2 * BLK)
-    for c in loads[:3]:
+    for c in loads[4:7]:
         c.wait()
-    prepare(0)
-    coefficients(PANELS - 1, 0)
     pl.semaphore_wait(bar, len(peers))
     send_z(range(Z_A))
     send_own()
+    prepare(0)
+    coefficients(PANELS - 1, 0)
     solve(0, {})
     stage2(0)
     forward_own(range(0, 4))
@@ -325,7 +330,7 @@
     for h in range(2):
         rs = slice(h * BLK, h * BLK + BLK)
         out_side[rs, :] = side_ref[rs, :] - apply(s_ref[rs, BLK:], t_ref[rs, BLK:], xw[0])
-    loads[3].wait()
+    loads[7].wait()
     for k in range(NCH):
         zwait(cp if k % 2 == 0 else cm, k)
     convert_all(0)
@@ -337,7 +342,13 @@
     forward_far(range(2, 3))
     stage3(1)
     send_far(range(Z_A + 3, NCH))
-    forward_far(range(3, 5))
+    forward_far(range(3, 8))
+    early = 2
+    for k in range(early):
+        zwait(qp if k % 2 == 0 else qm, k)
+        zwait(q2, k)
+        convert(2, k)
+        convert(3, k)
     stage4(1)
     gather_x()
     for h in range(2):
@@ -348,12 +359,11 @@
         out_side[rs, :] = jnp.where(jnp.broadcast_to(slots[0] == here, (BLK, 128)), xw[0], new)
 
     for k in range(NCH):
-        if 5 <= k + 4 < NCH:
-            forward_far([k + 4])
-        zwait(qp if k % 2 == 0 else qm, k)
-        zwait(q2, k)
-        convert(2, k)
-        convert(3, k)
+        if k >= early:
+            zwait(qp if k % 2 == 0 else qm, k)
+            zwait(q2, k)
+            convert(2, k)
+            convert(3, k)
         product(k)
     for n, (p, k) in enumerate(zsends):
         pltpu.make_async_copy(piece(p, k), piece(p, k), zs.at[n]).wait()
@@ -368,9 +378,13 @@
     sides, prod = pl.pallas_call(
         kernel,
         out_shape=(jax.ShapeDtypeStruct((512, 128), F32), jax.ShapeDtypeStruct((ORD, 128), F32)),
-        in_specs=[vm] * 4 + [pl.BlockSpec(memory_space=pltpu.HBM)] * 4,
+        in_specs=[pl.BlockSpec(memory_space=pltpu.HBM)] * 8,
         out_specs=(vm, vm),
         scratch_shapes=[
+            pltpu.VMEM((1, 64), jnp.int32),
+            pltpu.VMEM((32, 128), F32),
+            pltpu.VMEM((32, 128), F32),
+            pltpu.VMEM((1, 128), jnp.int32),
             pltpu.VMEM((512, 128), F32),
             pltpu.VMEM((512, 512), F32),
             pltpu.VMEM((512, 512), F32),
@@ -391,7 +405,7 @@
             pltpu.VMEM((8, 128), F32),
             dma((8, NCH)), dma((7 * NCH,)),
             dma((2, 8)), dma((2, 8)), dma((2, 4)), dma((2, 4)), dma((2, 8)), dma((2, 8)),
-            dma((4,)),
+            dma((8,)),
         ],
         compiler_params=pltpu.CompilerParams(
             collective_id=0, has_side_effects=True, vmem_limit_bytes=48 << 20

time: 55.6 us -> 53.8 us (0.968)
  Pallas kernels: 53 us -> 51.2 us
    pallas_call x1, Pallas kernels: 53 us -> 51.2 us  [on_device(): pl.pallas_call(kernel, out_shape=(jax.ShapeDtypeStruct((512, 128), F32),...]
where the time goes in v4:
time: 53.8 us; the launch traced here: 53.7 us
  Pallas kernels  51.2 us (95%)
  other arithmetic  1.08 us (2%)
  local copies, waits for them, and re-layouts  0.71 us (1%)
  between operations  0.66 us (1%)
    pallas_call x1, Pallas kernels, on_device(): pl.pallas_call(kernel, out_shape=(jax.ShapeDtypeStruct((512, 128), F32),...  51.2 us
    add x1, other arithmetic, on_device(): return (sides, vectors + prod)  1.08 us

profile of v4, /device:TPU:1, one launch (start us, length us, event | category | flops | bytes accessed | tf_op | source)
XLA Modules:
  0.0 53.7 jit_solution(16738624117427939398)
XLA Ops:
  0.6 0.0 copy-start
  0.6 51.2 %shard_map.104 = (f32[512,128]{1,0:T(8,128)S(1)}, f32[2048,128]{1,0:T(8,128)S(1)}) custom-call(s32[1,64]{1,0:T(1,128)} %bitcast.10, f32[32,128]{1,0:T(8,128)} %bitcast.8, f32[32,128]{1,0:T(8,128)} %bitcast.9, s32[1,128]{1,0:T(1,128)} %bitcast.11, f32[512,128]{1,0:T(8,128)} %side_hbm.1, f32[512,512]{1,0:T(8,128)} %s_hbm.1, f32[512,512]{1,0:T(8,128)} %t_hbm.1, ...), custom_call_target="tpu_custom_call" | custom-call | tf_op jit(solution)/shard_map/pallas_call | solution.py:378
  51.9 0.0 copy-done
  51.9 1.1 %add.3 = f32[2048,128]{1,0:T(8,128)} add(f32[2048,128]{1,0:T(8,128)S(1)} %copy-done, f32[2048,128]{1,0:T(8,128)S(1)} %get-tuple-element.5) | non-fusion elementwise | flops 262144 | bytes 3145728 | tf_op jit(solution)/shard_map/add | solution.py:419
  53.0 0.7 %copy.12 = f32[512,128]{1,0:T(8,128)} copy(f32[512,128]{1,0:T(8,128)S(1)} %get-tuple-element.8) | data formatting | bytes 524288
Async XLA Ops:
  0.6 51.2 %copy-start = (f32[2048,128]{1,0:T(8,128)S(1)}, f32[2048,128]{1,0:T(8,128)}, u32[]{:S(2)}) copy-start(f32[2048,128]{1,0:T(8,128)} %param.17) | copy-start | bytes 3145732

commit v5 on v4

--- a/solution.py
+++ b/solution.py
@@ -325,8 +325,9 @@
     stage4(0)
     rbuf[...] -= apply(half(s_ref, 1, right), half(t_ref, 1, right), xw[0])
     solve(1, {})
+    send_far(range(Z_A, Z_A + 1))
     stage2(1)
-    send_far(range(Z_A, Z_A + 2))
+    send_far(range(Z_A + 1, Z_A + 2))
     for h in range(2):
         rs = slice(h * BLK, h * BLK + BLK)
         out_side[rs, :] = side_ref[rs, :] - apply(s_ref[rs, BLK:], t_ref[rs, BLK:], xw[0])

time: 53.8 us -> 52.9 us (0.983)
  Pallas kernels: 51.2 us -> 50.2 us
    pallas_call x1, Pallas kernels: 51.2 us -> 50.2 us  [on_device(): pl.pallas_call(kernel, out_shape=(jax.ShapeDtypeStruct((512, 128), F32),...]
where the time goes in v5:
time: 52.9 us; the launch traced here: 52.6 us
  Pallas kernels  50.2 us (95%)
  other arithmetic  1.08 us (2%)
  local copies, waits for them, and re-layouts  0.71 us (1%)
  between operations  0.66 us (1%)
    pallas_call x1, Pallas kernels, on_device(): pl.pallas_call(kernel, out_shape=(jax.ShapeDtypeStruct((512, 128), F32),...  50.2 us
    add x1, other arithmetic, on_device(): return (sides, vectors + prod)  1.08 us

profile of v5, /device:TPU:1, one launch (start us, length us, event | category | flops | bytes accessed | tf_op | source)
XLA Modules:
  0.0 52.6 jit_solution(5446566121170532163)
XLA Ops:
  0.6 0.0 copy-start
  0.6 50.2 %shard_map.104 = (f32[512,128]{1,0:T(8,128)S(1)}, f32[2048,128]{1,0:T(8,128)S(1)}) custom-call(s32[1,64]{1,0:T(1,128)} %bitcast.10, f32[32,128]{1,0:T(8,128)} %bitcast.8, f32[32,128]{1,0:T(8,128)} %bitcast.9, s32[1,128]{1,0:T(1,128)} %bitcast.11, f32[512,128]{1,0:T(8,128)} %side_hbm.1, f32[512,512]{1,0:T(8,128)} %s_hbm.1, f32[512,512]{1,0:T(8,128)} %t_hbm.1, ...), custom_call_target="tpu_custom_call" | custom-call | tf_op jit(solution)/shard_map/pallas_call | solution.py:379
  50.9 0.0 copy-done
  50.9 1.1 %add.3 = f32[2048,128]{1,0:T(8,128)} add(f32[2048,128]{1,0:T(8,128)S(1)} %copy-done, f32[2048,128]{1,0:T(8,128)S(1)} %get-tuple-element.5) | non-fusion elementwise | flops 262144 | bytes 3145728 | tf_op jit(solution)/shard_map/add | solution.py:420
  51.9 0.7 %copy.12 = f32[512,128]{1,0:T(8,128)} copy(f32[512,128]{1,0:T(8,128)S(1)} %get-tuple-element.8) | data formatting | bytes 524288
Async XLA Ops:
  0.6 50.2 %copy-start = (f32[2048,128]{1,0:T(8,128)S(1)}, f32[2048,128]{1,0:T(8,128)}, u32[]{:S(2)}) copy-start(f32[2048,128]{1,0:T(8,128)} %param.17) | copy-start | bytes 3145732
